TPU v7x, 32 devices: a whole 2x2x4 slice. The times are simulated.
32 devices in a mesh: xy: 16 (over z, y, core), gz: 2 (over x).
Axes of the slice: x: 2, y: 2, z: 4, core: 2. Of those that a mesh axis runs over, the one named last changes fastest.
Arguments:
- hidden_features: bfloat16 [16, 16, 16, 512], P('gz', None, 'xy'), may hold values from -6 to 6
- scaling_factors_prenormal: float32 [512], replicated, may hold values from 0.1 to 1.9
- attention_input_matrices: bfloat16 [3, 512, 1536], P(None, 'xy'), may hold values from -1 to 1
- final_projection_matrices: bfloat16 [3, 512, 512], P(None, 'xy'), may hold values from -0.25 to 0.25
- score_scaling: float32 [3, 8], replicated, may hold values from 0 to 40
- filled_pillar_positions: int32 [16, 16], P('xy'), may hold values from 0 to 15, as said below
- filled_pillar_totals: int32 [16], P('xy'), may hold values from 4 to 16, as said below
Outputs:
- block_out: bfloat16 [16, 16, 16, 512], P('gz', None, 'xy')
Inputs may be any that keep to these rules, and one draw needn't show every extreme that they name: Row t of filled_pillar_positions is a permutation of 0 to 15; an entry c names the column x = c, y = t. `filled_pillar_totals`: some tile has all of its 16 columns occupied.
All inputs are finite; a program needn't handle non-finite values.
Results may differ from a plain program's by a relative error of at most 0.012.
Values may be sent and summed in bfloat16 or wider, within the bound.
No kernel may reach another device: no remote copies, remote signals or barrier semaphores. Data moves between devices by JAX's collectives and lax.ppermute only.
A program may use at most 64 MiB of HBM per device.

v0:
```python
import math
import jax
import jax.numpy as jnp
from jax import lax
from jax.sharding import PartitionSpec as P

EPSILON = 1e-06


def rms_scale(vector_rows):
    return vector_rows * lax.rsqrt(
        jnp.mean(vector_rows * vector_rows, axis=-1, keepdims=True) + EPSILON
    )


def project_qkv(tokens_in, w_project, attention_parts_number):
    projected = jnp.dot(tokens_in, w_project, preferred_element_type=jnp.float32)
    outer_shape = projected.shape[:-1]
    channels = w_project.shape[0]
    split_rows = projected.reshape(
        outer_shape + (3, attention_parts_number, channels // attention_parts_number)
    )
    queries = (
        rms_scale(split_rows[..., 0, :, :]).reshape(outer_shape + (channels,)).astype(jnp.bfloat16)
    )
    key_rows = (
        rms_scale(split_rows[..., 1, :, :]).reshape(outer_shape + (channels,)).astype(jnp.bfloat16)
    )
    values = split_rows[..., 2, :, :].reshape(outer_shape + (channels,)).astype(jnp.bfloat16)
    return (queries, key_rows, values)


def softmax_over_fibers(queries, key_rows, values, temper_row):
    attention_parts_number = temper_row.shape[0]
    outer_size, query_len, inner_size, channels = queries.shape
    key_len = key_rows.shape[1]
    head_dim = channels // attention_parts_number
    query_heads = queries.reshape(
        outer_size, query_len, inner_size, attention_parts_number, head_dim
    )
    key_heads = key_rows.reshape(outer_size, key_len, inner_size, attention_parts_number, head_dim)
    value_heads = values.reshape(outer_size, key_len, inner_size, attention_parts_number, head_dim)
    scores = jnp.einsum(
        "anbhd,ambhd->abhnm", query_heads, key_heads, preferred_element_type=jnp.float32
    )
    scores = scores * (temper_row / math.sqrt(head_dim))[None, None, :, None, None]
    weights = jax.nn.softmax(scores, axis=-1).astype(jnp.bfloat16)
    mixture = jnp.einsum(
        "abhnm,ambhd->anbhd", weights, value_heads, preferred_element_type=jnp.float32
    )
    return mixture.astype(jnp.bfloat16).reshape(outer_size, query_len, inner_size, channels)


def out_project(mixture, w_back):
    return jnp.dot(mixture, w_back, preferred_element_type=jnp.float32).astype(jnp.bfloat16)


def shards(
    hidden_features,
    scaling_factors_prenormal,
    attention_input_matrices,
    final_projection_matrices,
    score_scaling,
    filled_pillar_positions,
    filled_pillar_totals,
):
    full_qkv, full_out = (
        lax.all_gather(attention_input_matrices, "xy", axis=1, tiled=True),
        lax.all_gather(final_projection_matrices, "xy", axis=1, tiled=True),
    )
    attention_parts_number = score_scaling.shape[1]
    x_local, z_cells, y_rows, channels = hidden_features.shape
    normed = (rms_scale(hidden_features.astype(jnp.float32)) * scaling_factors_prenormal).astype(
        jnp.bfloat16
    )
    y_lines = normed.reshape(x_local * z_cells, y_rows, channels)
    local_query, local_keys, local_values = project_qkv(
        y_lines, full_qkv[1], attention_parts_number
    )
    query_along_y, keys_along_y, values_along_y = (
        lax.all_to_all(local_query, "xy", split_axis=0, concat_axis=1, tiled=True),
        lax.all_to_all(local_keys, "xy", split_axis=0, concat_axis=1, tiled=True),
        lax.all_to_all(local_values, "xy", split_axis=0, concat_axis=1, tiled=True),
    )
    y_mix = softmax_over_fibers(
        query_along_y[:, :, None, :],
        keys_along_y[:, :, None, :],
        values_along_y[:, :, None, :],
        score_scaling[1],
    )[:, :, 0, :]
    second_direction_answer = lax.all_to_all(
        out_project(y_mix, full_out[1]), "xy", split_axis=1, concat_axis=0, tiled=True
    ).reshape(hidden_features.shape)
    pieces = project_qkv(
        lax.all_to_all(normed, "gz", split_axis=1, concat_axis=0, tiled=True),
        full_qkv[0],
        attention_parts_number,
    )
    full_len, slab_part, items, _ = pieces[0].shape
    shaped = (1, full_len, slab_part * items, channels)
    x_mix = softmax_over_fibers(
        pieces[0].reshape(shaped),
        pieces[1].reshape(shaped),
        pieces[2].reshape(shaped),
        score_scaling[0],
    )
    result_rows = out_project(x_mix, full_out[0]).reshape(full_len, slab_part, items, channels)
    first_direction_answer = lax.all_to_all(
        result_rows, "gz", split_axis=0, concat_axis=1, tiled=True
    )
    cols_here = x_local * y_rows
    total_cols = filled_pillar_positions.shape[1]
    my_cols = lax.axis_index("gz") * cols_here + jnp.arange(cols_here, dtype=jnp.int32)
    live_rank = jnp.arange(total_cols, dtype=jnp.int32) < filled_pillar_totals[0]
    matches = filled_pillar_positions[0][None, :] == my_cols[:, None]
    live = jnp.any(jnp.logical_and(matches, live_rank[None, :]), axis=1)
    vertical_asking_terms, vertical_matching_terms, vertical_content_terms = project_qkv(
        normed, full_qkv[2], attention_parts_number
    )
    vertical_blended = softmax_over_fibers(
        vertical_asking_terms, vertical_matching_terms, vertical_content_terms, score_scaling[2]
    )
    z_full = out_project(vertical_blended, full_out[2])
    live_grid = live.reshape(x_local, 1, y_rows, 1)
    vertical_answer = jnp.where(live_grid, z_full, jnp.zeros_like(z_full))
    summed = (
        hidden_features.astype(jnp.float32)
        + first_direction_answer.astype(jnp.float32)
        + second_direction_answer.astype(jnp.float32)
    )
    summed = summed + vertical_answer.astype(jnp.float32)
    return summed.astype(jnp.bfloat16)


def solution(mesh):
    in_specs = (
        P("gz", None, "xy", None),
        P(),
        P(None, "xy", None),
        P(None, "xy", None),
        P(),
        P("xy", None),
        P("xy"),
    )
    out_specs = P("gz", None, "xy", None)
    return jax.shard_map(shards, mesh=mesh, in_specs=in_specs, out_specs=out_specs, check_vma=False)
```

profile of v0, /device:TPU:0, one launch (start us, length us, event | category | flops | bytes accessed | tf_op | source)
XLA Modules:
  0.0 148.3 jit_solution(13666185661406171766)
XLA Ops:
  6.5 0.7 all-gather.3.cloned.1.call-update
  7.3 1.0 fusion.23
  8.3 1.0 fusion.25
  9.3 0.7 copy.102
  10.0 4.2 %all-to-all-start = ((bf16[8,16,1,512]{3,0,2,1:T(8,128)(2,1)}), bf16[8,16,1,512]{3,0,2,1:T(8,128)(2,1)S(1)}, u32[]{:S(2)}, u32[]{:S(2)}) async-start(bf16[8,16,1,512]{3,0,2,1:T(8,128)(2,1)} %copy.102), calls=%async_computation | async-start | bytes 262144 | tf_op jit(solution)/shard_map/all_to_all | solution.py:95
  14.3 0.7 all-gather.5.cloned.1.call-update
  15.0 0.8 multiply_bitcast_fusion.2
  16.5 0.8 and_reduce_fusion
  17.3 1.5 %all-to-all-done = bf16[8,16,1,512]{3,0,2,1:T(8,128)(2,1)S(1)} async-done(((bf16[8,16,1,512]{3,0,2,1:T(8,128)(2,1)}), bf16[8,16,1,512]{3,0,2,1:T(8,128)(2,1)S(1)}, u32[]{:S(2)}, u32[]{:S(2)}) %all-to-all-start) | async-done | bytes 131104 | tf_op jit(solution)/shard_map/all_to_all | solution.py:95
  18.8 0.7 copy.103
  19.5 46.0 %all-gather.3.cloned.1.call-done = bf16[3,512,1536]{2,1,0:T(8,128)(2,1)} async-done(((bf16[3,32,1536]{2,1,0:T(8,128)(2,1)}), bf16[3,512,1536]{2,1,0:T(8,128)(2,1)}) %all-gather.3.cloned.1.call-update) | async-done | bytes 4718608 | tf_op jit(solution)/shard_map/all_gather | solution.py:68
  65.5 4.4 %slice_bitcast_fusion.2 = (bf16[1536,512]{0,1:T(8,128)(2,1)}, bf16[1536,512]{0,1:T(8,128)(2,1)S(1)}, bf16[1536,512]{0,1:T(8,128)(2,1)}) fusion(bf16[3,512,1536]{2,1,0:T(8,128)(2,1)} %all-gather.3.cloned.1.call-done), kind=kLoop, calls=%fused_computation.5 | loop fusion | bytes 9437184 | tf_op jit(solution)/shard_map/dot_general | solution.py:17
  69.9 1.7 %copy.104 = bf16[1536,512]{1,0:T(8,128)(2,1)S(1)} copy(bf16[1536,512]{0,1:T(8,128)(2,1)} %get-tuple-element.11) | data formatting | bytes 3145728 | tf_op jit(solution)/shard_map/dot_general | solution.py:17
  71.6 2.6 %copy.112 = bf16[1536,512]{1,0:T(8,128)(2,1)} copy(bf16[1536,512]{0,1:T(8,128)(2,1)} %get-tuple-element.13) | data formatting | bytes 3145728 | tf_op jit(solution)/shard_map/dot_general | solution.py:17
  74.3 2.0 %convolution_bitcast_fusion.2 = f32[128,1,3,8,64]{0,4,3,2,1:T(8,128)S(1)} fusion(bf16[128,512,1,1]{1,0,3,2:T(8,128)(2,1)S(1)} %bitcast.200, bf16[3,8,64,512]{3,2,1,0:T(8,128)(2,1)} %bitcast.199), kind=kOutput, calls=%fused_computation.8 | convolution fusion | flops 201326592 | bytes 2490368 | tf_op jit(solution)/shard_map/dot_general | solution.py:17
  76.3 0.9 copy-done
  77.3 0.5 broadcast.203
  77.8 1.2 reduce.26
  79.0 1.0 copy.180
  80.1 0.7 reshape.552
  80.8 3.5 %all-to-all-start.3 = ((bf16[16,2,2048]{2,1,0:T(2,128)(2,1)}), bf16[16,2,2048]{2,1,0:T(2,128)(2,1)S(1)}, u32[]{:S(2)}, u32[]{:S(2)}) async-start(bf16[16,2,2048]{2,1,0:T(2,128)(2,1)} %reshape.552), calls=%async_computation.3 | async-start | bytes 262144 | tf_op jit(solution)/shard_map/all_to_all | solution.py:81
  84.3 1.8 %convolution_bitcast_fusion.1 = f32[16,8,1,3,8,64]{5,1,4,3,0,2:T(8,128)S(1)} fusion(bf16[16,8,512,1,1]{2,1,4,3,0:T(8,128)(2,1)} %bitcast.207, bf16[3,8,64,512,1]{3,2,1,0,4:T(8,128)(2,1)S(1)} %bitcast.197), kind=kOutput, calls=%fused_computation.7 | convolution fusion | flops 201326592 | bytes 2490368 | tf_op jit(solution)/shard_map/dot_general | solution.py:17
  86.1 0.4 multiply_reduce_fusion.3
  86.5 0.4 fusion.22
  86.9 0.8 fusion.60
  87.7 1.0 fusion.9
  88.7 0.6 reduce.25
  89.3 0.1 copy.179
  89.4 0.7 reshape.550
  90.1 0.7 copy.125
  90.8 0.9 convolution_bitcast_fusion
  91.8 0.4 all-to-all-done.3
  92.2 5.8 %all-to-all-start.4 = ((bf16[16,2,2048]{2,1,0:T(2,128)(2,1)}), bf16[16,2,2048]{2,1,0:T(2,128)(2,1)S(1)}, u32[]{:S(2)}, u32[]{:S(2)}) async-start(bf16[16,2,2048]{2,1,0:T(2,128)(2,1)} %reshape.550), calls=%async_computation.4 | async-start | bytes 262144 | tf_op jit(solution)/shard_map/all_to_all | solution.py:82
  97.9 0.3 multiply_reduce_fusion.1
  98.3 1.0 slice.122
  99.3 0.2 reshape.524
  99.6 0.6 reduce.27
  100.1 0.1 copy.181
  100.3 0.7 reshape.554
  101.0 5.2 %all-to-all-done.4 = bf16[16,2,2048]{2,1,0:T(2,128)(2,1)S(1)} async-done(((bf16[16,2,2048]{2,1,0:T(2,128)(2,1)}), bf16[16,2,2048]{2,1,0:T(2,128)(2,1)S(1)}, u32[]{:S(2)}, u32[]{:S(2)}) %all-to-all-start.4) | async-done | bytes 131104 | tf_op jit(solution)/shard_map/all_to_all | solution.py:82
  106.2 3.5 %all-to-all-start.2 = ((bf16[16,2,2048]{2,1,0:T(2,128)(2,1)}), bf16[16,2,2048]{2,1,0:T(2,128)(2,1)S(1)}, u32[]{:S(2)}, u32[]{:S(2)}) async-start(bf16[16,2,2048]{2,1,0:T(2,128)(2,1)} %reshape.554), calls=%async_computation.2 | async-start | bytes 262144 | tf_op jit(solution)/shard_map/all_to_all | solution.py:83
  109.8 2.0 %fusion.54 = (f32[8,8,16]{2,1,0:T(8,128)}, f32[8,8,16,16]{2,3,1,0:T(8,128)}) fusion(f32[8,16,1,3,8,64]{5,1,4,3,0,2:T(8,128)S(1)} %convolution_bitcast_fusion, f32[8]{0:T(128)S(1)} %get-tuple-element.19, f32[8,16,8]{1,2,0:T(8,128)S(1)} %get-tuple-element.27, f32[8,16,8]{1,2,0:T(8,128)S(1)} %get-tuple-element.28), kind=kOutput, calls=%fused_computation.99 | convolution fusion | flops 2408463 | bytes 1184256 | tf_op jit(solution)/shard_map/sub | solution.py:47
  111.7 0.1 reshape.553
  111.9 0.2 reshape.548
  112.1 0.1 reshape.551
  112.2 0.2 reshape.549
  112.4 5.2 %all-to-all-done.2 = bf16[16,2,2048]{2,1,0:T(2,128)(2,1)S(1)} async-done(((bf16[16,2,2048]{2,1,0:T(2,128)(2,1)}), bf16[16,2,2048]{2,1,0:T(2,128)(2,1)S(1)}, u32[]{:S(2)}, u32[]{:S(2)}) %all-to-all-start.2) | async-done | bytes 131104 | tf_op jit(solution)/shard_map/all_to_all | solution.py:83
  117.6 0.1 reshape.555
  117.8 0.2 reshape.547
  118.0 0.5 fusion.55
  118.5 0.3 fusion.10
  118.8 0.1 copy.123
  118.9 0.2 squeeze_reshape.3
  119.1 1.3 convolution_convert_fusion.4
  120.4 0.7 copy.124
  121.2 3.6 %all-to-all-start.5 = ((bf16[8,16,512]{2,0,1:T(8,128)(2,1)}), bf16[8,16,512]{2,0,1:T(8,128)(2,1)S(1)}, u32[]{:S(2)}, u32[]{:S(2)}) async-start(bf16[8,16,512]{2,0,1:T(8,128)(2,1)} %copy.124), calls=%async_computation.5 | async-start | bytes 262144 | tf_op jit(solution)/shard_map/all_to_all | solution.py:91
  124.8 1.3 fusion.11
  126.1 0.1 copy.127
  126.2 0.2 reshape.533
  126.4 0.9 fusion.12
  127.3 5.3 %all-to-all-done.5 = bf16[8,16,512]{2,0,1:T(8,128)(2,1)S(1)} async-done(((bf16[8,16,512]{2,0,1:T(8,128)(2,1)}), bf16[8,16,512]{2,0,1:T(8,128)(2,1)S(1)}, u32[]{:S(2)}, u32[]{:S(2)}) %all-to-all-start.5) | async-done | bytes 131104 | tf_op jit(solution)/shard_map/all_to_all | solution.py:91
  132.7 3.4 %all-to-all-start.1 = ((bf16[16,8,1,512]{3,1,2,0:T(8,128)(2,1)}), bf16[16,8,1,512]{3,1,2,0:T(8,128)(2,1)S(1)}, u32[]{:S(2)}, u32[]{:S(2)}) async-start(bf16[16,8,1,512]{3,1,2,0:T(8,128)(2,1)} %fusion.12), calls=%async_computation.1 | async-start | bytes 262144 | tf_op jit(solution)/shard_map/all_to_all | solution.py:108
  136.1 4.4 %all-to-all-done.1 = bf16[16,8,1,512]{3,1,2,0:T(8,128)(2,1)S(1)} async-done(((bf16[16,8,1,512]{3,1,2,0:T(8,128)(2,1)}), bf16[16,8,1,512]{3,1,2,0:T(8,128)(2,1)S(1)}, u32[]{:S(2)}, u32[]{:S(2)}) %all-to-all-start.1) | async-done | bytes 131104 | tf_op jit(solution)/shard_map/all_to_all | solution.py:108
  140.5 0.9 fusion.18
  (29 shorter events, 0.5 us)
Async XLA Ops:
  6.5 59.0 %all-gather.3.cloned.1.call-start = ((), (), s32[]{:S(2)}) async-start(), calls=%async_computation.6 | async-start | bytes 5013504 | tf_op jit(solution)/shard_map/all_gather | solution.py:68
  10.0 8.8 %all-to-all-start = ((bf16[8,16,1,512]{3,0,2,1:T(8,128)(2,1)}), bf16[8,16,1,512]{3,0,2,1:T(8,128)(2,1)S(1)}, u32[]{:S(2)}, u32[]{:S(2)}) async-start(bf16[8,16,1,512]{3,0,2,1:T(8,128)(2,1)} %copy.102), calls=%async_computation | async-start | bytes 262144 | tf_op jit(solution)/shard_map/all_to_all | solution.py:95
  14.3 104.9 %all-gather.5.cloned.1.call-start = ((), (), s32[]{:S(2)}) async-start(), calls=%async_computation.7 | async-start | bytes 1671168 | tf_op jit(solution)/shard_map/all_gather | solution.py:69
  76.2 0.9 copy-start
  80.8 11.4 %all-to-all-start.3 = ((bf16[16,2,2048]{2,1,0:T(2,128)(2,1)}), bf16[16,2,2048]{2,1,0:T(2,128)(2,1)S(1)}, u32[]{:S(2)}, u32[]{:S(2)}) async-start(bf16[16,2,2048]{2,1,0:T(2,128)(2,1)} %reshape.552), calls=%async_computation.3 | async-start | bytes 262144 | tf_op jit(solution)/shard_map/all_to_all | solution.py:81
  91.7 7.5 %copy-start.3 = (bf16[1,16,8,8,64]{4,1,3,2,0:T(8,128)(2,1)S(1)}, bf16[1,16,8,8,64]{4,1,3,2,0:T(8,128)(2,1)}, u32[]{:S(2)}) copy-start(bf16[1,16,8,8,64]{4,1,3,2,0:T(8,128)(2,1)} %fusion.9) | copy-start | bytes 393220
  92.2 14.1 %all-to-all-start.4 = ((bf16[16,2,2048]{2,1,0:T(2,128)(2,1)}), bf16[16,2,2048]{2,1,0:T(2,128)(2,1)S(1)}, u32[]{:S(2)}, u32[]{:S(2)}) async-start(bf16[16,2,2048]{2,1,0:T(2,128)(2,1)} %reshape.550), calls=%async_computation.4 | async-start | bytes 262144 | tf_op jit(solution)/shard_map/all_to_all | solution.py:82
  106.2 11.4 %all-to-all-start.2 = ((bf16[16,2,2048]{2,1,0:T(2,128)(2,1)}), bf16[16,2,2048]{2,1,0:T(2,128)(2,1)S(1)}, u32[]{:S(2)}, u32[]{:S(2)}) async-start(bf16[16,2,2048]{2,1,0:T(2,128)(2,1)} %reshape.554), calls=%async_computation.2 | async-start | bytes 262144 | tf_op jit(solution)/shard_map/all_to_all | solution.py:83
  118.8 6.0 %copy-start.4 = (f32[8,8,16]{2,1,0:T(8,128)S(1)}, f32[8,8,16]{2,1,0:T(8,128)}, u32[]{:S(2)}) copy-start(f32[8,8,16]{2,1,0:T(8,128)} %get-tuple-element.21) | copy-start | bytes 12292
  121.1 5.3 %copy-start.2 = (bf16[3,512,512]{2,1,0:T(8,128)(2,1)S(1)}, bf16[3,512,512]{2,1,0:T(8,128)(2,1)}, u32[]{:S(2)}) copy-start(bf16[3,512,512]{2,1,0:T(8,128)(2,1)} %all-gather.5.cloned.1.call-done) | copy-start | bytes 4718596
  121.2 11.5 %all-to-all-start.5 = ((bf16[8,16,512]{2,0,1:T(8,128)(2,1)}), bf16[8,16,512]{2,0,1:T(8,128)(2,1)S(1)}, u32[]{:S(2)}, u32[]{:S(2)}) async-start(bf16[8,16,512]{2,0,1:T(8,128)(2,1)} %copy.124), calls=%async_computation.5 | async-start | bytes 262144 | tf_op jit(solution)/shard_map/all_to_all | solution.py:91
  126.1 14.4 %copy-start.1 = (bf16[8,16,1,512]{3,1,2,0:T(8,128)(2,1)S(1)}, bf16[8,16,1,512]{3,1,2,0:T(8,128)(2,1)}, u32[]{:S(2)}) copy-start(bf16[8,16,1,512]{3,1,2,0:T(8,128)(2,1)} %param.7) | copy-start | bytes 393220
  132.7 7.8 %all-to-all-start.1 = ((bf16[16,8,1,512]{3,1,2,0:T(8,128)(2,1)}), bf16[16,8,1,512]{3,1,2,0:T(8,128)(2,1)S(1)}, u32[]{:S(2)}, u32[]{:S(2)}) async-start(bf16[16,8,1,512]{3,1,2,0:T(8,128)(2,1)} %fusion.12), calls=%async_computation.1 | async-start | bytes 262144 | tf_op jit(solution)/shard_map/all_to_all | solution.py:108
Sparse Core Ops, SparseCore 0:
  9.6 55.8 all-gather.2
  67.7 39.1 all-gather.4
where the time goes:
time: 149 us; the launch traced here: 148 us
  waiting for transfers between devices  69.6 us (47%)
  starting transfers between devices  24.1 us (16%)
  local copies, waits for them, and re-layouts  19.2 us (13%)
  between operations  14.4 us (10%)
  matrix products  13.7 us (9%)
  other arithmetic  7.31 us (5%)
    all_gather x1, waiting for transfers between devices, shards(): lax.all_gather(attention_input_matrices, 'xy', axis=1, tiled=True)  46 us
    dot_general x4, local copies, waits for them, and re-layouts, project_qkv(): jnp.dot(tokens_in, w_project, preferred_element_type=jnp.float32)  9.41 us
    all_to_all x1, starting transfers between devices, shards(): lax.all_to_all(local_keys, 'xy', split_axis=0, concat_axis=1, tiled=True)  5.78 us
    all_to_all x1, waiting for transfers between devices, shards(): lax.all_to_all(out_project(y_mix, full_out[1]), 'xy', split_axis=1, conca...  5.35 us
    all_to_all x1, waiting for transfers between devices, shards(): lax.all_to_all(local_keys, 'xy', split_axis=0, concat_axis=1, tiled=True)  5.24 us
    all_to_all x1, waiting for transfers between devices, shards(): lax.all_to_all(local_values, 'xy', split_axis=0, concat_axis=1, tiled=True)  5.21 us
    dot_general x3, matrix products, project_qkv(): jnp.dot(tokens_in, w_project, preferred_element_type=jnp.float32)  4.68 us
    unnamed x22, local copies, waits for them, and re-layouts  4.68 us
  transfers between devices with their start and end apart: 8, of which 7 were waited for; matrix products, arithmetic and copies ran while one was open for 25% of the time, Pallas kernels for 0%

commit v1 on v0

--- a/solution.py
+++ b/solution.py
@@ -5,6 +5,24 @@
 from jax.sharding import PartitionSpec as P
 
 EPSILON = 1e-06
+
+
+def enter_strings_for(z, axis_k, arr):
+    spare = z.shape
+    current_value = z.reshape(*spare[:axis_k], arr, spare[axis_k] // arr, *spare[axis_k + 1 :])
+    arr_now = jnp.moveaxis(current_value, axis_k, 0)
+    return arr_now
+
+
+def carry_the_sectors(s0, array_axis):
+    s0 = jnp.moveaxis(s0, 0, array_axis)
+    long_array = s0.shape
+    even = s0.reshape(
+        *long_array[:array_axis],
+        long_array[array_axis] * long_array[array_axis + 1],
+        *long_array[array_axis + 2 :]
+    )
+    return even
 
 
 def rms_scale(vector_rows):
@@ -88,9 +106,26 @@
         values_along_y[:, :, None, :],
         score_scaling[1],
     )[:, :, 0, :]
-    second_direction_answer = lax.all_to_all(
-        out_project(y_mix, full_out[1]), "xy", split_axis=1, concat_axis=0, tiled=True
-    ).reshape(hidden_features.shape)
+
+    def set_the_sector(view, which_axis, xx, u):
+        piece_next = lax.axis_size(which_axis)
+        a_now, everything = (piece_next, lax.axis_index(which_axis))
+        q_next = enter_strings_for(view, xx, a_now)
+        leaves = [q_next[everything]]
+        for q in [*range(1, a_now)]:
+            row_out = q_next[everything ^ q]
+            block_now = lax.ppermute(
+                row_out, axis_name=which_axis, perm=[(idx, idx ^ q) for idx in range(a_now)]
+            )
+            leaves.append(block_now)
+        near = jnp.stack(leaves, axis=0)
+        q_next = near[everything ^ jnp.arange(a_now)]
+        clean = carry_the_sectors(q_next, u)
+        return clean
+
+    second_direction_answer = set_the_sector(out_project(y_mix, full_out[1]), "xy", 1, 0).reshape(
+        hidden_features.shape
+    )
     pieces = project_qkv(
         lax.all_to_all(normed, "gz", split_axis=1, concat_axis=0, tiled=True),
         full_qkv[0],

time: 149 us -> 159 us (1.067)
  starting transfers between devices: 24.1 us -> 41.7 us
  waiting for transfers between devices: 69.6 us -> 62.6 us
  matrix products: 13.7 us -> 12 us
    ppermute x0 -> x15, starting transfers between devices: none -> 20.9 us  [set_the_sector(): lax.ppermute(row_out, axis_name=which_axis, perm=[(idx, idx ^ q) for idx...]
    all_to_all x1 -> x0, waiting for transfers between devices: 5.35 us -> none  [shards(): lax.all_to_all(out_project(y_mix, full_out[1]), 'xy', split_axis=1, conca...]
    all_to_all x1, waiting for transfers between devices: 4.43 us -> 0.01 us  [shards(): lax.all_to_all(result_rows, 'gz', split_axis=0, concat_axis=1, tiled=True)]
    all_to_all x1 -> x0, starting transfers between devices: 3.64 us -> none  [shards(): lax.all_to_all(out_project(y_mix, full_out[1]), 'xy', split_axis=1, conca...]
    ppermute x0 -> x15, waiting for transfers between devices: none -> 2.51 us  [set_the_sector(): lax.ppermute(row_out, axis_name=which_axis, perm=[(idx, idx ^ q) for idx...]
    all_to_all x1, waiting for transfers between devices: 5.24 us -> 7.1 us  [shards(): lax.all_to_all(local_keys, 'xy', split_axis=0, concat_axis=1, tiled=True)]
    unnamed x22 -> x37, local copies, waits for them, and re-layouts: 4.68 us -> 5.54 us
  transfers between devices with their start and end apart: 8 -> 22, of which waited for: 7 -> 7; matrix products, arithmetic and copies ran while one was open for 25% -> 23% of each run, Pallas kernels for 0% -> 0%
where the time goes in v1:
time: 159 us
  waiting for transfers between devices  62.6 us (39%)
  starting transfers between devices  41.7 us (26%)
  local copies, waits for them, and re-layouts  19.8 us (12%)
  between operations  14.7 us (9%)
  matrix products  12 us (8%)
  other arithmetic  7.85 us (5%)
    all_gather x1, waiting for transfers between devices, shards(): lax.all_gather(attention_input_matrices, 'xy', axis=1, tiled=True)  46 us
    ppermute x15, starting transfers between devices, set_the_sector(): lax.ppermute(row_out, axis_name=which_axis, perm=[(idx, idx ^ q) for idx...  20.9 us
    dot_general x4, local copies, waits for them, and re-layouts, project_qkv(): jnp.dot(tokens_in, w_project, preferred_element_type=jnp.float32)  8.8 us
    all_to_all x1, waiting for transfers between devices, shards(): lax.all_to_all(local_keys, 'xy', split_axis=0, concat_axis=1, tiled=True)  7.1 us
    all_to_all x1, starting transfers between devices, shards(): lax.all_to_all(local_keys, 'xy', split_axis=0, concat_axis=1, tiled=True)  6.02 us
    unnamed x37, local copies, waits for them, and re-layouts  5.54 us
    dot_general x3, matrix products, project_qkv(): jnp.dot(tokens_in, w_project, preferred_element_type=jnp.float32)  5.28 us
    all_to_all x1, waiting for transfers between devices, shards(): lax.all_to_all(local_values, 'xy', split_axis=0, concat_axis=1, tiled=True)  4.64 us
  transfers between devices with their start and end apart: 22, of which 7 were waited for; matrix products, arithmetic and copies ran while one was open for 23% of the time, Pallas kernels for 0%

profile of v1, /device:TPU:0, one launch (start us, length us, event | category | flops | bytes accessed | tf_op | source)
XLA Modules:
  0.0 158.7 jit_solution(6821034297756731035)
XLA Ops:
  6.5 0.7 all-gather.3.cloned.1.call-update
  7.3 1.0 fusion.23
  8.3 1.0 fusion.25
  9.3 0.7 copy.529
  10.0 4.2 %all-to-all-start = ((bf16[8,16,1,512]{3,0,2,1:T(8,128)(2,1)}), bf16[8,16,1,512]{3,0,2,1:T(8,128)(2,1)S(1)}, u32[]{:S(2)}, u32[]{:S(2)}) async-start(bf16[8,16,1,512]{3,0,2,1:T(8,128)(2,1)} %copy.529), calls=%async_computation | async-start | bytes 262144 | tf_op jit(solution)/shard_map/all_to_all | solution.py:130
  14.3 0.7 all-gather.5.cloned.1.call-update
  15.1 1.3 multiply_bitcast_fusion.2
  17.1 0.8 and_reduce_fusion
  18.0 0.9 all-to-all-done
  18.8 0.7 copy.530
  19.5 46.0 %all-gather.3.cloned.1.call-done = bf16[3,512,1536]{2,1,0:T(8,128)(2,1)} async-done(((bf16[3,32,1536]{2,1,0:T(8,128)(2,1)}), bf16[3,512,1536]{2,1,0:T(8,128)(2,1)}) %all-gather.3.cloned.1.call-update) | async-done | bytes 4718608 | tf_op jit(solution)/shard_map/all_gather | solution.py:86
  65.5 3.9 %slice_bitcast_fusion.2 = (bf16[1536,512]{0,1:T(8,128)(2,1)S(1)}, bf16[1536,512]{0,1:T(8,128)(2,1)S(1)}, bf16[1536,512]{0,1:T(8,128)(2,1)}) fusion(bf16[3,512,1536]{2,1,0:T(8,128)(2,1)} %all-gather.3.cloned.1.call-done), kind=kLoop, calls=%fused_computation.6 | loop fusion | bytes 9437184 | tf_op jit(solution)/shard_map/dot_general | solution.py:35
  69.4 2.6 %copy.539 = bf16[1536,512]{1,0:T(8,128)(2,1)} copy(bf16[1536,512]{0,1:T(8,128)(2,1)} %get-tuple-element.13) | data formatting | bytes 3145728 | tf_op jit(solution)/shard_map/dot_general | solution.py:35
  72.0 2.0 %convolution_bitcast_fusion.2 = f32[128,1,3,8,64]{0,4,3,2,1:T(8,128)S(1)} fusion(bf16[128,512,1,1]{1,0,3,2:T(8,128)(2,1)S(1)} %bitcast.231, bf16[3,8,64,512]{3,2,1,0:T(8,128)(2,1)} %bitcast.230), kind=kOutput, calls=%fused_computation.9 | convolution fusion | flops 201326592 | bytes 2490368 | tf_op jit(solution)/shard_map/dot_general | solution.py:35
  74.0 0.9 copy-done
  75.1 0.5 broadcast.238
  75.6 1.3 reduce.26
  76.9 1.0 copy.638
  77.9 0.7 reshape.639
  78.6 3.5 %all-to-all-start.3 = ((bf16[16,2,2048]{2,1,0:T(2,128)(2,1)}), bf16[16,2,2048]{2,1,0:T(2,128)(2,1)S(1)}, u32[]{:S(2)}, u32[]{:S(2)}) async-start(bf16[16,2,2048]{2,1,0:T(2,128)(2,1)} %reshape.639), calls=%async_computation.3 | async-start | bytes 262144 | tf_op jit(solution)/shard_map/all_to_all | solution.py:99
  82.1 1.6 %copy.531 = bf16[1536,512]{1,0:T(8,128)(2,1)} copy(bf16[1536,512]{0,1:T(8,128)(2,1)S(1)} %get-tuple-element.11) | data formatting | bytes 3145728 | tf_op jit(solution)/shard_map/dot_general | solution.py:35
  83.7 0.7 copy.551
  84.4 2.4 %convolution_bitcast_fusion.1 = f32[16,8,1,3,8,64]{5,1,4,3,0,2:T(8,128)S(1)} fusion(bf16[16,8,512,1,1]{2,1,4,3,0:T(8,128)(2,1)} %bitcast.237, bf16[3,8,64,512,1]{3,2,1,0,4:T(8,128)(2,1)} %bitcast.229), kind=kOutput, calls=%fused_computation.8 | convolution fusion | flops 201326592 | bytes 2490368 | tf_op jit(solution)/shard_map/dot_general | solution.py:35
  86.8 0.4 multiply_reduce_fusion.3
  87.2 0.4 fusion.22
  87.6 0.8 fusion.61
  88.4 1.0 fusion.9
  89.4 0.9 convolution_bitcast_fusion
  90.4 0.3 multiply_reduce_fusion.1
  90.7 1.0 slice.124
  91.8 0.6 reduce.25
  92.5 0.7 reshape.637
  93.2 0.6 reduce.27
  93.9 0.7 reshape.641
  94.7 0.2 reshape.600
  95.0 6.0 %all-to-all-start.4 = ((bf16[16,2,2048]{2,1,0:T(2,128)(2,1)}), bf16[16,2,2048]{2,1,0:T(2,128)(2,1)S(1)}, u32[]{:S(2)}, u32[]{:S(2)}) async-start(bf16[16,2,2048]{2,1,0:T(2,128)(2,1)} %reshape.637), calls=%async_computation.4 | async-start | bytes 262144 | tf_op jit(solution)/shard_map/all_to_all | solution.py:100
  101.0 0.8 fusion.55
  101.8 7.1 %all-to-all-done.4 = bf16[16,2,2048]{2,1,0:T(2,128)(2,1)S(1)} async-done(((bf16[16,2,2048]{2,1,0:T(2,128)(2,1)}), bf16[16,2,2048]{2,1,0:T(2,128)(2,1)S(1)}, u32[]{:S(2)}, u32[]{:S(2)}) %all-to-all-start.4) | async-done | bytes 131104 | tf_op jit(solution)/shard_map/all_to_all | solution.py:100
  108.9 3.5 %all-to-all-start.2 = ((bf16[16,2,2048]{2,1,0:T(2,128)(2,1)}), bf16[16,2,2048]{2,1,0:T(2,128)(2,1)S(1)}, u32[]{:S(2)}, u32[]{:S(2)}) async-start(bf16[16,2,2048]{2,1,0:T(2,128)(2,1)} %reshape.641), calls=%async_computation.2 | async-start | bytes 262144 | tf_op jit(solution)/shard_map/all_to_all | solution.py:101
  112.4 0.3 fusion.11
  113.0 1.9 %fusion.12 = bf16[16,8,1,512]{3,1,2,0:T(8,128)(2,1)} fusion(bf16[16,8,512]{2,1,0:T(8,128)(2,1)S(1)} %reshape.600, bf16[3,512,512]{2,1,0:T(8,128)(2,1)} %all-gather.5.cloned.1.call-done), kind=kOutput, calls=%fused_computation.28 | convolution fusion | flops 67174400 | bytes 786432 | tf_op jit(solution)/shard_map/dot_general | solution.py:73
  115.6 4.6 %all-to-all-done.2 = bf16[16,2,2048]{2,1,0:T(2,128)(2,1)S(1)} async-done(((bf16[16,2,2048]{2,1,0:T(2,128)(2,1)}), bf16[16,2,2048]{2,1,0:T(2,128)(2,1)S(1)}, u32[]{:S(2)}, u32[]{:S(2)}) %all-to-all-start.2) | async-done | bytes 131104 | tf_op jit(solution)/shard_map/all_to_all | solution.py:101
  120.3 3.6 %all-to-all-start.1 = ((bf16[16,8,1,512]{3,1,2,0:T(8,128)(2,1)}), bf16[16,8,1,512]{3,1,2,0:T(8,128)(2,1)S(1)}, u32[]{:S(2)}, u32[]{:S(2)}) async-start(bf16[16,8,1,512]{3,1,2,0:T(8,128)(2,1)} %fusion.12), calls=%async_computation.1 | async-start | bytes 262144 | tf_op jit(solution)/shard_map/all_to_all | solution.py:143
  124.2 0.5 fusion.56
  124.7 0.3 fusion.10
  125.1 0.2 squeeze_reshape.3
  125.3 0.8 copy-done.3
  126.1 0.2 convolution_convert_fusion.4
  126.4 0.4 constant_dynamic-slice_fusion
  127.0 1.8 %collective-permute-start.2 = (bf16[8,1,512]{2,1,0:T(2,128)(2,1)S(1)}, bf16[8,1,512]{2,1,0:T(2,128)(2,1)S(1)}, u32[]{:S(2)}, u32[]{:S(2)}) collective-permute-start(bf16[8,1,512]{2,1,0:T(2,128)(2,1)S(1)} %get-tuple-element.30), channel_id=1, source_target_pairs={{0,6},{2,4},{4,2},{6,0},{8,14},{10,12},{12,10},{14,8},{16,22},{18,... | collective-permute-start | bytes 24584 | tf_op jit(solution)/shard_map/ppermute | solution.py:117
  128.7 1.7 %collective-permute-start.4 = (bf16[8,1,512]{2,1,0:T(2,128)(2,1)S(1)}, bf16[8,1,512]{2,1,0:T(2,128)(2,1)S(1)}, u32[]{:S(2)}, u32[]{:S(2)}) collective-permute-start(bf16[8,1,512]{2,1,0:T(2,128)(2,1)S(1)} %get-tuple-element.28), channel_id=1, source_target_pairs={{0,10},{2,8},{4,14},{6,12},{8,2},{10,0},{12,6},{14,4},{16,26},{18,... | collective-permute-start | bytes 24584 | tf_op jit(solution)/shard_map/ppermute | solution.py:117
  130.7 2.5 %collective-permute-start.6 = (bf16[8,1,512]{2,1,0:T(2,128)(2,1)S(1)}, bf16[8,1,512]{2,1,0:T(2,128)(2,1)S(1)}, u32[]{:S(2)}, u32[]{:S(2)}) collective-permute-start(bf16[8,1,512]{2,1,0:T(2,128)(2,1)S(1)} %get-tuple-element.26), channel_id=1, source_target_pairs={{0,14},{2,12},{4,10},{6,8},{8,6},{10,4},{12,2},{14,0},{16,30},{18,... | collective-permute-start | bytes 24584 | tf_op jit(solution)/shard_map/ppermute | solution.py:117
  133.2 0.4 collective-permute-start.7
  133.6 2.4 %collective-permute-start.8 = (bf16[8,1,512]{2,1,0:T(2,128)(2,1)S(1)}, bf16[8,1,512]{2,1,0:T(2,128)(2,1)S(1)}, u32[]{:S(2)}, u32[]{:S(2)}) collective-permute-start(bf16[8,1,512]{2,1,0:T(2,128)(2,1)S(1)} %get-tuple-element.24), channel_id=1, source_target_pairs={{0,18},{2,16},{4,22},{6,20},{8,26},{10,24},{12,30},{14,28},{16,2},... | collective-permute-start | bytes 24584 | tf_op jit(solution)/shard_map/ppermute | solution.py:117
  136.0 0.3 collective-permute-start.9
  136.3 3.3 %collective-permute-start.10 = (bf16[8,1,512]{2,1,0:T(2,128)(2,1)S(1)}, bf16[8,1,512]{2,1,0:T(2,128)(2,1)S(1)}, u32[]{:S(2)}, u32[]{:S(2)}) collective-permute-start(bf16[8,1,512]{2,1,0:T(2,128)(2,1)S(1)} %get-tuple-element.22), channel_id=1, source_target_pairs={{0,22},{2,20},{4,18},{6,16},{8,30},{10,28},{12,26},{14,24},{16,6},... | collective-permute-start | bytes 24584 | tf_op jit(solution)/shard_map/ppermute | solution.py:117
  139.7 0.7 collective-permute-start.11
  140.4 2.9 %collective-permute-start.12 = (bf16[8,1,512]{2,1,0:T(2,128)(2,1)S(1)}, bf16[8,1,512]{2,1,0:T(2,128)(2,1)S(1)}, u32[]{:S(2)}, u32[]{:S(2)}) collective-permute-start(bf16[8,1,512]{2,1,0:T(2,128)(2,1)S(1)} %get-tuple-element.20), channel_id=1, source_target_pairs={{0,26},{2,24},{4,30},{6,28},{8,18},{10,16},{12,22},{14,20},{16,10}... | collective-permute-start | bytes 24584 | tf_op jit(solution)/shard_map/ppermute | solution.py:117
  143.3 1.1 collective-permute-start.13
  144.4 3.5 %collective-permute-start.14 = (bf16[8,1,512]{2,1,0:T(2,128)(2,1)S(1)}, bf16[8,1,512]{2,1,0:T(2,128)(2,1)S(1)}, u32[]{:S(2)}, u32[]{:S(2)}) collective-permute-start(bf16[8,1,512]{2,1,0:T(2,128)(2,1)S(1)} %get-tuple-element.18), channel_id=1, source_target_pairs={{0,30},{2,28},{4,26},{6,24},{8,22},{10,20},{12,18},{14,16},{16,14}... | collective-permute-start | bytes 24584 | tf_op jit(solution)/shard_map/ppermute | solution.py:117
  148.0 1.8 %collective-permute-done.13 = bf16[8,1,512]{2,1,0:T(2,128)(2,1)S(1)} collective-permute-done((bf16[8,1,512]{2,1,0:T(2,128)(2,1)S(1)}, bf16[8,1,512]{2,1,0:T(2,128)(2,1)S(1)}, u32[]{:S(2)}, u32[]{:S(2)}) %collective-permute-start.13) | collective-permute-done | bytes 8224 | tf_op jit(solution)/shard_map/ppermute | solution.py:117
  149.8 0.5 collective-permute-done.14
  150.3 0.6 gather_fusion
  150.9 0.9 fusion.18
  (75 shorter events, 2.4 us)
Async XLA Ops:
  6.5 59.0 %all-gather.3.cloned.1.call-start = ((), (), s32[]{:S(2)}) async-start(), calls=%async_computation.5 | async-start | bytes 5013504 | tf_op jit(solution)/shard_map/all_gather | solution.py:86
  10.0 8.8 %all-to-all-start = ((bf16[8,16,1,512]{3,0,2,1:T(8,128)(2,1)}), bf16[8,16,1,512]{3,0,2,1:T(8,128)(2,1)S(1)}, u32[]{:S(2)}, u32[]{:S(2)}) async-start(bf16[8,16,1,512]{3,0,2,1:T(8,128)(2,1)} %copy.529), calls=%async_computation | async-start | bytes 262144 | tf_op jit(solution)/shard_map/all_to_all | solution.py:130
  14.3 98.7 %all-gather.5.cloned.1.call-start = ((), (), s32[]{:S(2)}) async-start(), calls=%async_computation.6 | async-start | bytes 1671168 | tf_op jit(solution)/shard_map/all_gather | solution.py:87
  74.0 0.9 copy-start
  78.6 16.4 %all-to-all-start.3 = ((bf16[16,2,2048]{2,1,0:T(2,128)(2,1)}), bf16[16,2,2048]{2,1,0:T(2,128)(2,1)S(1)}, u32[]{:S(2)}, u32[]{:S(2)}) async-start(bf16[16,2,2048]{2,1,0:T(2,128)(2,1)} %reshape.639), calls=%async_computation.3 | async-start | bytes 262144 | tf_op jit(solution)/shard_map/all_to_all | solution.py:99
  86.8 0.8 copy-start.4
  90.3 4.3 %copy-start.2 = (bf16[1,16,8,8,64]{4,1,3,2,0:T(8,128)(2,1)S(1)}, bf16[1,16,8,8,64]{4,1,3,2,0:T(8,128)(2,1)}, u32[]{:S(2)}) copy-start(bf16[1,16,8,8,64]{4,1,3,2,0:T(8,128)(2,1)} %fusion.9) | copy-start | bytes 393220
  95.0 13.9 %all-to-all-start.4 = ((bf16[16,2,2048]{2,1,0:T(2,128)(2,1)}), bf16[16,2,2048]{2,1,0:T(2,128)(2,1)S(1)}, u32[]{:S(2)}, u32[]{:S(2)}) async-start(bf16[16,2,2048]{2,1,0:T(2,128)(2,1)} %reshape.637), calls=%async_computation.4 | async-start | bytes 262144 | tf_op jit(solution)/shard_map/all_to_all | solution.py:100
  108.9 11.4 %all-to-all-start.2 = ((bf16[16,2,2048]{2,1,0:T(2,128)(2,1)}), bf16[16,2,2048]{2,1,0:T(2,128)(2,1)S(1)}, u32[]{:S(2)}, u32[]{:S(2)}) async-start(bf16[16,2,2048]{2,1,0:T(2,128)(2,1)} %reshape.641), calls=%async_computation.2 | async-start | bytes 262144 | tf_op jit(solution)/shard_map/all_to_all | solution.py:101
  120.3 30.6 %all-to-all-start.1 = ((bf16[16,8,1,512]{3,1,2,0:T(8,128)(2,1)}), bf16[16,8,1,512]{3,1,2,0:T(8,128)(2,1)S(1)}, u32[]{:S(2)}, u32[]{:S(2)}) async-start(bf16[16,8,1,512]{3,1,2,0:T(8,128)(2,1)} %fusion.12), calls=%async_computation.1 | async-start | bytes 262144 | tf_op jit(solution)/shard_map/all_to_all | solution.py:143
  124.7 1.4 copy-start.3
  125.0 25.9 %copy-start.1 = (bf16[8,16,1,512]{3,1,2,0:T(8,128)(2,1)S(1)}, bf16[8,16,1,512]{3,1,2,0:T(8,128)(2,1)}, u32[]{:S(2)}) copy-start(bf16[8,16,1,512]{3,1,2,0:T(8,128)(2,1)} %param.7) | copy-start | bytes 393220
  126.8 3.7 %collective-permute-start = (bf16[8,1,512]{2,1,0:T(2,128)(2,1)S(1)}, bf16[8,1,512]{2,1,0:T(2,128)(2,1)S(1)}, u32[]{:S(2)}, u32[]{:S(2)}) collective-permute-start(bf16[8,1,512]{2,1,0:T(2,128)(2,1)S(1)} %get-tuple-element.32), channel_id=1, source_target_pairs={{0,2},{2,0},{4,6},{6,4},{8,10},{10,8},{12,14},{14,12},{16,18},{18,... | collective-permute-start | bytes 24584 | tf_op jit(solution)/shard_map/ppermute | solution.py:117
  126.9 3.8 %collective-permute-start.1 = (bf16[8,1,512]{2,1,0:T(2,128)(2,1)S(1)}, bf16[8,1,512]{2,1,0:T(2,128)(2,1)S(1)}, u32[]{:S(2)}, u32[]{:S(2)}) collective-permute-start(bf16[8,1,512]{2,1,0:T(2,128)(2,1)S(1)} %get-tuple-element.31), channel_id=1, source_target_pairs={{0,4},{2,6},{4,0},{6,2},{8,12},{10,14},{12,8},{14,10},{16,20},{18,... | collective-permute-start | bytes 24584 | tf_op jit(solution)/shard_map/ppermute | solution.py:117
  127.0 6.2 %collective-permute-start.2 = (bf16[8,1,512]{2,1,0:T(2,128)(2,1)S(1)}, bf16[8,1,512]{2,1,0:T(2,128)(2,1)S(1)}, u32[]{:S(2)}, u32[]{:S(2)}) collective-permute-start(bf16[8,1,512]{2,1,0:T(2,128)(2,1)S(1)} %get-tuple-element.30), channel_id=1, source_target_pairs={{0,6},{2,4},{4,2},{6,0},{8,14},{10,12},{12,10},{14,8},{16,22},{18,... | collective-permute-start | bytes 24584 | tf_op jit(solution)/shard_map/ppermute | solution.py:117
  128.7 4.9 %collective-permute-start.3 = (bf16[8,1,512]{2,1,0:T(2,128)(2,1)S(1)}, bf16[8,1,512]{2,1,0:T(2,128)(2,1)S(1)}, u32[]{:S(2)}, u32[]{:S(2)}) collective-permute-start(bf16[8,1,512]{2,1,0:T(2,128)(2,1)S(1)} %get-tuple-element.29), channel_id=1, source_target_pairs={{0,8},{2,10},{4,12},{6,14},{8,0},{10,2},{12,4},{14,6},{16,24},{18,... | collective-permute-start | bytes 24584 | tf_op jit(solution)/shard_map/ppermute | solution.py:117
  128.7 7.2 %collective-permute-start.4 = (bf16[8,1,512]{2,1,0:T(2,128)(2,1)S(1)}, bf16[8,1,512]{2,1,0:T(2,128)(2,1)S(1)}, u32[]{:S(2)}, u32[]{:S(2)}) collective-permute-start(bf16[8,1,512]{2,1,0:T(2,128)(2,1)S(1)} %get-tuple-element.28), channel_id=1, source_target_pairs={{0,10},{2,8},{4,14},{6,12},{8,2},{10,0},{12,6},{14,4},{16,26},{18,... | collective-permute-start | bytes 24584 | tf_op jit(solution)/shard_map/ppermute | solution.py:117
  130.5 5.9 %collective-permute-start.5 = (bf16[8,1,512]{2,1,0:T(2,128)(2,1)S(1)}, bf16[8,1,512]{2,1,0:T(2,128)(2,1)S(1)}, u32[]{:S(2)}, u32[]{:S(2)}) collective-permute-start(bf16[8,1,512]{2,1,0:T(2,128)(2,1)S(1)} %get-tuple-element.27), channel_id=1, source_target_pairs={{0,12},{2,14},{4,8},{6,10},{8,4},{10,6},{12,0},{14,2},{16,28},{18,... | collective-permute-start | bytes 24584 | tf_op jit(solution)/shard_map/ppermute | solution.py:117
  130.7 9.0 %collective-permute-start.6 = (bf16[8,1,512]{2,1,0:T(2,128)(2,1)S(1)}, bf16[8,1,512]{2,1,0:T(2,128)(2,1)S(1)}, u32[]{:S(2)}, u32[]{:S(2)}) collective-permute-start(bf16[8,1,512]{2,1,0:T(2,128)(2,1)S(1)} %get-tuple-element.26), channel_id=1, source_target_pairs={{0,14},{2,12},{4,10},{6,8},{8,6},{10,4},{12,2},{14,0},{16,30},{18,... | collective-permute-start | bytes 24584 | tf_op jit(solution)/shard_map/ppermute | solution.py:117
  133.2 7.2 %collective-permute-start.7 = (bf16[8,1,512]{2,1,0:T(2,128)(2,1)S(1)}, bf16[8,1,512]{2,1,0:T(2,128)(2,1)S(1)}, u32[]{:S(2)}, u32[]{:S(2)}) collective-permute-start(bf16[8,1,512]{2,1,0:T(2,128)(2,1)S(1)} %get-tuple-element.25), channel_id=1, source_target_pairs={{0,16},{2,18},{4,20},{6,22},{8,24},{10,26},{12,28},{14,30},{16,0},... | collective-permute-start | bytes 24584 | tf_op jit(solution)/shard_map/ppermute | solution.py:117
  133.6 9.7 %collective-permute-start.8 = (bf16[8,1,512]{2,1,0:T(2,128)(2,1)S(1)}, bf16[8,1,512]{2,1,0:T(2,128)(2,1)S(1)}, u32[]{:S(2)}, u32[]{:S(2)}) collective-permute-start(bf16[8,1,512]{2,1,0:T(2,128)(2,1)S(1)} %get-tuple-element.24), channel_id=1, source_target_pairs={{0,18},{2,16},{4,22},{6,20},{8,26},{10,24},{12,30},{14,28},{16,2},... | collective-permute-start | bytes 24584 | tf_op jit(solution)/shard_map/ppermute | solution.py:117
  136.0 8.5 %collective-permute-start.9 = (bf16[8,1,512]{2,1,0:T(2,128)(2,1)S(1)}, bf16[8,1,512]{2,1,0:T(2,128)(2,1)S(1)}, u32[]{:S(2)}, u32[]{:S(2)}) collective-permute-start(bf16[8,1,512]{2,1,0:T(2,128)(2,1)S(1)} %get-tuple-element.23), channel_id=1, source_target_pairs={{0,20},{2,22},{4,16},{6,18},{8,28},{10,30},{12,24},{14,26},{16,4},... | collective-permute-start | bytes 24584 | tf_op jit(solution)/shard_map/ppermute | solution.py:117
  136.3 11.6 %collective-permute-start.10 = (bf16[8,1,512]{2,1,0:T(2,128)(2,1)S(1)}, bf16[8,1,512]{2,1,0:T(2,128)(2,1)S(1)}, u32[]{:S(2)}, u32[]{:S(2)}) collective-permute-start(bf16[8,1,512]{2,1,0:T(2,128)(2,1)S(1)} %get-tuple-element.22), channel_id=1, source_target_pairs={{0,22},{2,20},{4,18},{6,16},{8,30},{10,28},{12,26},{14,24},{16,6},... | collective-permute-start | bytes 24584 | tf_op jit(solution)/shard_map/ppermute | solution.py:117
  139.7 8.3 %collective-permute-start.11 = (bf16[8,1,512]{2,1,0:T(2,128)(2,1)S(1)}, bf16[8,1,512]{2,1,0:T(2,128)(2,1)S(1)}, u32[]{:S(2)}, u32[]{:S(2)}) collective-permute-start(bf16[8,1,512]{2,1,0:T(2,128)(2,1)S(1)} %get-tuple-element.21), channel_id=1, source_target_pairs={{0,24},{2,26},{4,28},{6,30},{8,16},{10,18},{12,20},{14,22},{16,8},... | collective-permute-start | bytes 24584 | tf_op jit(solution)/shard_map/ppermute | solution.py:117
  140.4 7.6 %collective-permute-start.12 = (bf16[8,1,512]{2,1,0:T(2,128)(2,1)S(1)}, bf16[8,1,512]{2,1,0:T(2,128)(2,1)S(1)}, u32[]{:S(2)}, u32[]{:S(2)}) collective-permute-start(bf16[8,1,512]{2,1,0:T(2,128)(2,1)S(1)} %get-tuple-element.20), channel_id=1, source_target_pairs={{0,26},{2,24},{4,30},{6,28},{8,18},{10,16},{12,22},{14,20},{16,10}... | collective-permute-start | bytes 24584 | tf_op jit(solution)/shard_map/ppermute | solution.py:117
  143.3 6.5 %collective-permute-start.13 = (bf16[8,1,512]{2,1,0:T(2,128)(2,1)S(1)}, bf16[8,1,512]{2,1,0:T(2,128)(2,1)S(1)}, u32[]{:S(2)}, u32[]{:S(2)}) collective-permute-start(bf16[8,1,512]{2,1,0:T(2,128)(2,1)S(1)} %get-tuple-element.19), channel_id=1, source_target_pairs={{0,28},{2,30},{4,24},{6,26},{8,20},{10,22},{12,16},{14,18},{16,12}... | collective-permute-start | bytes 24584 | tf_op jit(solution)/shard_map/ppermute | solution.py:117
  144.4 5.9 %collective-permute-start.14 = (bf16[8,1,512]{2,1,0:T(2,128)(2,1)S(1)}, bf16[8,1,512]{2,1,0:T(2,128)(2,1)S(1)}, u32[]{:S(2)}, u32[]{:S(2)}) collective-permute-start(bf16[8,1,512]{2,1,0:T(2,128)(2,1)S(1)} %get-tuple-element.18), channel_id=1, source_target_pairs={{0,30},{2,28},{4,26},{6,24},{8,22},{10,20},{12,18},{14,16},{16,14}... | collective-permute-start | bytes 24584 | tf_op jit(solution)/shard_map/ppermute | solution.py:117
Sparse Core Ops, SparseCore 0:
  9.6 55.8 all-gather.2
  67.7 39.2 all-gather.4
